TPU v7x, 512 devices: a whole 4x4x16 slice. The times are simulated.
512 devices in a mesh: grp: 16 (over y, x), tok: 32 (over z, core).
Axes of the slice: x: 4, y: 4, z: 16, core: 2. Of those that a mesh axis runs over, the one named last changes fastest.
Arguments:
- hidden_in: bfloat16 [16, 4096, 1024], P('grp', 'tok'), may hold values from -6 to 6
- lengths: int32 [16, 3], P('grp'), may hold values from 1 to 3072, 4096 in all within a row
- prefix_cache: bfloat16 [16, 512, 512], P('grp', 'tok'), may hold values from -2600 to 2600
- routes: int32 [16, 4096, 8], P('grp', 'tok'), may hold values from 0 to 31, all different within a row; in each aligned block of 128 rows (0 to 127, 128 to 255, ..., all dimensions but the last counted through in order) at most 40 rows name the same one
- gates: float32 [16, 4096, 8], P('grp', 'tok'), may hold values from 0.05 to 0.4
- attn_gain: float32 [1024], replicated, may hold values from 0.1 to 1.9
- w_qkv: bfloat16 [1024, 1024], P('grp', 'tok'), may hold values from -0.75 to 0.75
- w_out: bfloat16 [512, 1024], P('grp', 'tok'), may hold values from -0.25 to 0.25
- moe_gain: float32 [1024], replicated, may hold values from 0.1 to 1.9
- expert_gate_up: bfloat16 [32, 1024, 1024], P('tok', 'grp'), may hold values from -0.1875 to 0.1875
- expert_down: bfloat16 [32, 512, 1024], P('tok', 'grp'), may hold values from -0.25 to 0.25
Outputs:
- hidden_out: bfloat16 [16, 4096, 1024], P('grp', 'tok')
- suffix_cache: bfloat16 [16, 4096, 512], P('grp', 'tok')
Inputs may be any that keep to these rules, and one draw needn't show every extreme that they name: Each group's 3 lengths sum to 4096; no request is longer than 3072 tokens, and some request of every draw has exactly 3072. `routes`: each token names 8 different experts. Among the 128 tokens of one device no expert is named more than 40 times, a bound that some block reaches.
All inputs are finite; a program needn't handle non-finite values.
Results may differ from a plain program's by a relative error of at most 0.02.
Values may be sent and summed in bfloat16 or wider, within the bound.
A program may use at most 128 MiB of HBM per device.

v0:
```python
import jax
import jax.numpy as jnp
from jax import lax
from jax.sharding import PartitionSpec as P

HEADS = 8
KV_HEADS = 4
HEAD_DIM = 64
FF = 512
EXPERTS = 32
TOP = 8
CAP = 40
epsilon = 1e-05
score_scale = 0.015625
rope_base = 10000.0
big_negative = -1e30


def rms_scale(values, gain):
    values = values.astype(jnp.float32)
    mean_square = jnp.mean(values * values, axis=-1, keepdims=True)
    return values * lax.rsqrt(mean_square + epsilon) * gain


def request_layout(group_lengths, token_index):
    ends = jnp.cumsum(group_lengths)
    starts = ends - group_lengths
    segment = jnp.sum((token_index[:, None] >= ends[None, :]).astype(jnp.int32), axis=1)
    match = segment[:, None] == jnp.arange(group_lengths.shape[0], dtype=jnp.int32)[None, :]
    offset = token_index - jnp.sum(jnp.where(match, starts[None, :], 0), axis=1)
    return (segment, offset)


def rotate(values, position):
    half_width = values.shape[-1] // 2
    frequency = rope_base ** (-jnp.arange(half_width, dtype=jnp.float32) * 2.0 / values.shape[-1])
    angle = position.astype(jnp.float32)[:, None] * frequency[None, :]
    cosine = jnp.cos(angle)[:, None, :]
    sine = jnp.sin(angle)[:, None, :]
    first = values[..., :half_width]
    second = values[..., half_width:]
    return jnp.concatenate(
        [first * cosine - second * sine, second * cosine + first * sine], axis=-1
    )


def attend(carry, grouped, keys_values, allowed):
    best, total, mixed = carry
    key_count = keys_values.shape[0]
    key_width = KV_HEADS * HEAD_DIM
    key_heads = keys_values[:, :key_width].reshape(key_count, KV_HEADS, HEAD_DIM).transpose(1, 0, 2)
    value_heads = (
        keys_values[:, key_width:].reshape(key_count, KV_HEADS, HEAD_DIM).transpose(1, 0, 2)
    )
    scores = (
        jnp.einsum("kqd,knd->kqn", grouped, key_heads, preferred_element_type=jnp.float32)
        * score_scale
    )
    if allowed is not None:
        row_count = grouped.shape[1]
        share = row_count // allowed.shape[0]
        mask = jnp.broadcast_to(allowed[:, None, :], (allowed.shape[0], share, key_count)).reshape(
            row_count, key_count
        )
        scores = jnp.where(mask[None], scores, big_negative)
    new_best = jnp.maximum(best, jnp.max(scores, axis=-1))
    factor = jnp.exp(best - new_best)
    probs = jnp.exp(scores - new_best[..., None])
    total = total * factor + jnp.sum(probs, axis=-1)
    mixed = mixed * factor[..., None] + jnp.einsum(
        "kqn,knd->kqd", probs.astype(jnp.bfloat16), value_heads, preferred_element_type=jnp.float32
    )
    return (new_best, total, mixed)


def local(
    hidden_in,
    lengths,
    prefix_cache,
    routes,
    gates,
    attn_gain,
    w_qkv,
    w_out,
    moe_gain,
    expert_gate_up,
    expert_down,
):
    tokens_here = hidden_in[0]
    tok_count = tokens_here.shape[0]
    axis_count = lax.axis_size("tok")
    device_place = lax.axis_index("tok")
    group_lengths = lengths[0]
    token_index = device_place * tok_count + jnp.arange(tok_count, dtype=jnp.int32)
    segment, offset = request_layout(group_lengths, token_index)
    position = prefix_cache.shape[1] * axis_count + offset
    query_width = HEADS * HEAD_DIM
    key_width = KV_HEADS * HEAD_DIM
    group_share = HEADS // KV_HEADS
    normed = rms_scale(tokens_here, attn_gain).astype(jnp.bfloat16)
    columns = lax.all_gather(w_qkv, "tok", axis=1, tiled=True)
    sliced = normed
    projected = jnp.dot(
        sliced,
        lax.all_gather(columns, "grp", axis=0, tiled=True),
        preferred_element_type=jnp.float32,
    )
    query = rotate(projected[:, :query_width].reshape(tok_count, HEADS, HEAD_DIM), position).astype(
        jnp.bfloat16
    )
    keys_new = rotate(
        projected[:, query_width : query_width + key_width].reshape(tok_count, KV_HEADS, HEAD_DIM),
        position,
    ).astype(jnp.bfloat16)
    values_new = projected[:, query_width + key_width :].astype(jnp.bfloat16)
    suffix_cache = jnp.concatenate([keys_new.reshape(tok_count, key_width), values_new], axis=1)
    row_count = tok_count * group_share
    grouped = (
        query.reshape(tok_count, KV_HEADS, group_share, HEAD_DIM)
        .transpose(1, 0, 2, 3)
        .reshape(KV_HEADS, row_count, HEAD_DIM)
    )
    start_carry = (
        jnp.full((KV_HEADS, row_count), big_negative, jnp.float32),
        jnp.zeros((KV_HEADS, row_count), jnp.float32),
        jnp.zeros((KV_HEADS, row_count, HEAD_DIM), jnp.float32),
    )
    carry = attend(
        start_carry, grouped, lax.all_gather(prefix_cache[0], "tok", axis=0, tiled=True), None
    )
    piece = lax.all_gather(suffix_cache, "tok", axis=0, tiled=True)
    key_index = jnp.arange(piece.shape[0], dtype=jnp.int32)
    key_segment, key_offset = request_layout(group_lengths, key_index)
    earlier = key_index[None, :] <= token_index[:, None]
    same_request = key_segment[None, :] == segment[:, None]
    carry = attend(carry, grouped, piece, earlier & same_request & (key_index[None, :] >= 0))
    best, total, mixed = carry
    attended = (mixed / total[..., None]).reshape(KV_HEADS, tok_count, group_share, HEAD_DIM)
    attended = attended.transpose(1, 0, 2, 3).reshape(tok_count, query_width).astype(jnp.bfloat16)
    out_columns = lax.all_gather(w_out, "tok", axis=1, tiled=True)
    sliced = attended
    projected_out = jnp.dot(
        sliced,
        lax.all_gather(out_columns, "grp", axis=0, tiled=True),
        preferred_element_type=jnp.float32,
    )
    after_attention = tokens_here.astype(jnp.float32) + projected_out
    moe_in = rms_scale(after_attention, moe_gain).astype(jnp.bfloat16)
    model_width = moe_in.shape[1]
    flat_routes = routes[0].reshape(-1)
    onehot = (flat_routes[:, None] == jnp.arange(EXPERTS, dtype=jnp.int32)[None, :]).astype(
        jnp.int32
    )
    slot_rank = jnp.sum(jnp.cumsum(onehot, axis=0) * onehot, axis=1) - 1
    slot_index = flat_routes * CAP + slot_rank
    source_token = jnp.arange(flat_routes.shape[0], dtype=jnp.int32) // TOP
    outgoing = (
        jnp.zeros((EXPERTS * CAP, model_width), jnp.bfloat16)
        .at[slot_index]
        .set(moe_in[source_token])
    )
    arrived = lax.all_to_all(
        outgoing.reshape(EXPERTS, CAP, model_width), "tok", split_axis=0, concat_axis=1, tiled=True
    )
    sliced = arrived
    hidden_pair = jnp.einsum(
        "erd,edf->erf",
        sliced,
        lax.all_gather(expert_gate_up, "grp", axis=1, tiled=True),
        preferred_element_type=jnp.float32,
    )
    activated = (jax.nn.silu(hidden_pair[..., :FF]) * hidden_pair[..., FF:]).astype(jnp.bfloat16)
    sliced = activated
    expert_result = jnp.einsum(
        "erf,efd->erd",
        sliced,
        lax.all_gather(expert_down, "grp", axis=1, tiled=True),
        preferred_element_type=jnp.float32,
    ).astype(jnp.bfloat16)
    returned = lax.all_to_all(
        expert_result, "tok", split_axis=1, concat_axis=0, tiled=True
    ).reshape(EXPERTS * CAP, -1)
    weighted = returned[slot_index].astype(jnp.float32) * gates[0].reshape(-1)[:, None]
    moe_out = jnp.sum(weighted.reshape(tok_count, TOP, -1), axis=1)
    hidden_out = (after_attention + moe_out).astype(jnp.bfloat16)
    return (hidden_out[None], suffix_cache[None])


def solution(mesh):
    return jax.shard_map(
        local,
        mesh=mesh,
        in_specs=(
            P("grp", "tok", None),
            P("grp", None),
            P("grp", "tok", None),
            P("grp", "tok", None),
            P("grp", "tok", None),
            P(),
            P("grp", "tok"),
            P("grp", "tok"),
            P(),
            P("tok", "grp", None),
            P("tok", "grp", None),
        ),
        out_specs=(P("grp", "tok", None), P("grp", "tok", None)),
        check_vma=False,
    )
```

profile of v0, /device:TPU:32, one launch (start us, length us, event | category | flops | bytes accessed | tf_op | source)
XLA Modules:
  0.0 593.4 jit_solution(6562197188762396571)
XLA Ops:
  7.2 35.0 %all_gather.24 = bf16[64,1024]{0,1:T(8,128)(2,1)S(1)} all-gather(bf16[64,32]{0,1:T(8,128)(2,1)} %param.17), channel_id=1, replica_groups=mesh['grp'=16,'tok'=32] {'tok'}, dimensions={1}, use_global_device_ids=true | all-gather | bytes 135168 | tf_op jit(solution)/shard_map/all_gather | solution.py:101
  46.1 55.2 %all-gather.7.cloned.1.call-done = bf16[1024,1024]{1,0:T(8,128)(2,1)} async-done(((bf16[64,1024]{1,0:T(8,128)(2,1)}), bf16[1024,1024]{1,0:T(8,128)(2,1)}) %all-gather.7.cloned.1.call-update) | async-done | bytes 2097168 | tf_op jit(solution)/shard_map/all_gather | solution.py:105
  101.3 2.2 fusion.30
  105.4 30.6 %all_gather.28 = bf16[32,1024]{0,1:T(8,128)(2,1)S(1)} all-gather(bf16[32,32]{0,1:T(8,128)(2,1)S(1)} %copy.120), channel_id=1, replica_groups=mesh['grp'=16,'tok'=32] {'tok'}, dimensions={1}, use_global_device_ids=true | all-gather | bytes 67584 | tf_op jit(solution)/shard_map/all_gather | solution.py:140
  137.7 2.4 broadcast_in_dim.41
  140.2 2.6 broadcast_in_dim.42
  142.7 31.0 %all-gather = bf16[1,512,512]{2,1,0:T(8,128)(2,1)S(1)} all-gather(bf16[1,16,512]{2,1,0:T(8,128)(2,1)S(1)} %copy-done.5), channel_id=2, replica_groups=mesh['grp'=16,'tok'=32] {'tok'}, dimensions={1}, use_global_device_ids=true | all-gather | bytes 540672 | tf_op jit(solution)/shard_map/all_gather | solution.py:129
  175.0 9.2 %reduce-window.11 = s32[32,8,128]{2,1,0:T(8,128)S(1)} reduce-window(s32[32,8,128]{2,1,0:T(8,128)S(1)} %fusion.37, s32[]{:T(128)} %constant.34.clone.1), window={size=1x1x128 pad=0_0x0_0x127_0}, to_apply=%region_9.10 | reduce-window | flops 4161536 | bytes 262148 | tf_op jit(solution)/shard_map/reduce-window.1
  186.0 1.8 multiply_reduce_fusion
  187.8 3.8 fusion.45
  191.6 2.9 copy.117
  194.6 2.9 copy.115
  197.5 3.5 fusion
  201.0 4.4 fusion.1
  205.4 1.9 copy-done
  207.9 11.2 %fusion.3 = f32[4,256,64]{1,2,0:T(8,128)} fusion(bf16[4,4096,64]{1,2,0:T(8,128)(2,1)} %bitcast.105, f32[4,256,4096]{2,1,0:T(8,128)} %copy-done, f32[4,256]{1,0:T(4,128)S(1)} %get-tuple-element.15, pred[256,4096]{1,0:T(8,128)(4,1)S(1)} %broadcast_in_dim.42), kind=kOutput, calls=%fused_computation.8 | convolution fusion | flops 553648128 | bytes 20189184 | tf_op jit(solution)/shard_map/kqn,knd->kqd/dot_general | solution.py:70
  221.0 16.5 %all-gather.11.cloned.1.call-done = bf16[512,1024]{1,0:T(8,128)(2,1)} async-done(((bf16[32,1024]{1,0:T(8,128)(2,1)}), bf16[512,1024]{1,0:T(8,128)(2,1)}) %all-gather.11.cloned.1.call-update) | async-done | bytes 1048592 | tf_op jit(solution)/shard_map/all_gather | solution.py:144
  239.3 14.7 %scatter_custom_fusion = bf16[1280,1024]{1,0:T(8,128)(2,1)} fusion(s32[1024]{0:T(1024)S(1)} %bitcast.118, bf16[128,1024]{1,0:T(8,128)(2,1)S(1)} %multiply_convert_fusion, s32[1024]{0:T(1024)S(1)} %broadcast_clamp_fusion.1, bf16[]{:T(256)} %constant.67.clone.1), kind=kCustom, calls=%fused_computation.19 | custom fusion | bytes 2621442 | tf_op jit(solution)/shard_map/scatter | solution.py:160
  254.1 12.8 %all-to-all-start = ((bf16[32,40,1024]{2,1,0:T(8,128)(2,1)}), bf16[32,40,1024]{2,1,0:T(8,128)(2,1)S(1)}, u32[]{:S(2)}, u32[]{:S(2)}) async-start(bf16[32,40,1024]{2,1,0:T(8,128)(2,1)} %bitcast.31), calls=%async_computation | async-start | bytes 5242880 | tf_op jit(solution)/shard_map/all_to_all | solution.py:162
  268.0 61.4 %all-gather.13.cloned.1.call-done = bf16[1,1024,1024]{2,1,0:T(8,128)(2,1)} async-done(((bf16[1,64,1024]{2,1,0:T(8,128)(2,1)}), bf16[1,1024,1024]{2,1,0:T(8,128)(2,1)}) %all-gather.13.cloned.1.call-update) | async-done | bytes 2097168 | tf_op jit(solution)/shard_map/all_gather | solution.py:169
  329.4 60.2 %all-to-all-done = bf16[32,40,1024]{2,1,0:T(8,128)(2,1)S(1)} async-done(((bf16[32,40,1024]{2,1,0:T(8,128)(2,1)}), bf16[32,40,1024]{2,1,0:T(8,128)(2,1)S(1)}, u32[]{:S(2)}, u32[]{:S(2)}) %all-to-all-start) | async-done | bytes 2621472 | tf_op jit(solution)/shard_map/all_to_all | solution.py:162
  389.6 6.2 %convolution_bitcast_fusion = f32[1,1280,1024]{2,1,0:T(8,128)} fusion(bf16[1280,1024]{1,0:T(8,128)(2,1)S(1)} %bitcast.104, bf16[1,1024,1024]{2,1,0:T(8,128)(2,1)} %all-gather.13.cloned.1.call-done), kind=kOutput, calls=%fused_computation.10 | convolution fusion | flops 2684354560 | bytes 9961472 | tf_op jit(solution)/shard_map/erd,edf->erf/dot_general | solution.py:166
  395.8 4.4 fusion.7
  400.2 18.2 %copy.137 = bf16[1,1280,1024]{2,0,1:T(2,128)(2,1)} copy(bf16[1,1280,1024]{2,1,0:T(8,128)(2,1)S(1)} %fusion.7) | data formatting | bytes 5242880 | tf_op jit(solution)/shard_map/convert_element_type | solution.py:179
  418.9 15.6 %reduce = bf16[1280,1024]{1,0:T(8,128)(2,1)S(1)} reduce(bf16[1280,1,1024]{2,1,0:T(2,128)(2,1)} %bitcast.99, bf16[]{:T(256)} %broadcast.297), dimensions={1}, to_apply=%bitcast.97.reduce_sub_computation | reduce | bytes 5242882
  434.4 3.0 reshape.386
  437.4 6.9 %all-to-all-start.1 = ((bf16[32,2,20480]{2,1,0:T(2,128)(2,1)}), bf16[32,2,20480]{2,1,0:T(2,128)(2,1)S(1)}, u32[]{:S(2)}, u32[]{:S(2)}) async-start(bf16[32,2,20480]{2,1,0:T(2,128)(2,1)} %reshape.386), calls=%async_computation.1 | async-start | bytes 5242880 | tf_op jit(solution)/shard_map/all_to_all | solution.py:180
  444.5 122.6 %all-to-all-done.1 = bf16[32,2,20480]{2,1,0:T(2,128)(2,1)S(1)} async-done(((bf16[32,2,20480]{2,1,0:T(2,128)(2,1)}), bf16[32,2,20480]{2,1,0:T(2,128)(2,1)S(1)}, u32[]{:S(2)}, u32[]{:S(2)}) %all-to-all-start.1) | async-done | bytes 2621472 | tf_op jit(solution)/shard_map/all_to_all | solution.py:180
  567.1 7.2 %reshape.387 = bf16[1280,1,1024]{2,1,0:T(2,128)(2,1)} reshape(bf16[32,2,20480]{2,1,0:T(2,128)(2,1)S(1)} %all-to-all-done.1) | data formatting | bytes 5242880
  574.3 3.5 copy.136
  577.8 5.4 gather_fusion
  583.2 2.9 fusion.6
  (94 shorter events, 17.1 us)
Async XLA Ops:
  7.2 94.1 %all-gather.7.cloned.1.call-start = ((), (), s32[]{:S(2)}) async-start(), calls=%async_computation.2 | async-start | bytes 2228224 | tf_op jit(solution)/shard_map/all_gather | solution.py:105
  42.3 63.1 %copy-start.7 = (bf16[32,32]{1,0:T(8,128)(2,1)S(1)}, bf16[32,32]{1,0:T(8,128)(2,1)}, u32[]{:S(2)}) copy-start(bf16[32,32]{1,0:T(8,128)(2,1)} %param.18) | copy-start | bytes 6148
  43.1 144.7 %all-gather.9.cloned.1.call-start = ((), (), s32[]{:S(2)}) async-start(), calls=%async_computation.3 | async-start | bytes 4325376 | tf_op jit(solution)/shard_map/all_gather | solution.py:131
  46.1 90.9 %copy-start.6 = (s32[1,128,8]{1,2,0:T(8,128)S(1)}, s32[1,128,8]{1,2,0:T(8,128)}, u32[]{:S(2)}) copy-start(s32[1,128,8]{1,2,0:T(8,128)} %param.14) | copy-start | bytes 12292
  103.5 0.8 copy-start.3
  105.3 132.3 %all-gather.11.cloned.1.call-start = ((), (), s32[]{:S(2)}) async-start(), calls=%async_computation.4 | async-start | bytes 1114112 | tf_op jit(solution)/shard_map/all_gather | solution.py:144
  137.7 5.0 copy-start.5
  142.7 42.0 %slice-start = ((f32[128,1024]{1,0:T(8,128)}), f32[128,512]{1,0:T(8,128)S(1)}, s32[]{:S(2)}) async-start(f32[128,1024]{1,0:T(8,128)} %copy-done.3), calls=%async_computation.7 | async-start | bytes 524288 | tf_op jit(solution)/shard_map/slice | solution.py:108
  201.0 6.3 %copy-start = (f32[4,256,4096]{2,1,0:T(8,128)}, f32[4,256,4096]{2,1,0:T(8,128)S(1)}, u32[]{:S(2)}) copy-start(f32[4,256,4096]{2,1,0:T(8,128)S(1)} %get-tuple-element.22) | copy-start | bytes 50331652
  201.0 6.3 %copy-start.1 = (f32[4,256,512]{2,1,0:T(8,128)S(1)}, f32[4,256,512]{2,1,0:T(8,128)}, u32[]{:S(2)}) copy-start(f32[4,256,512]{2,1,0:T(8,128)} %get-tuple-element.20) | copy-start | bytes 6291460
  207.9 11.2 %copy-start.4 = (bf16[512,256]{0,1:T(8,128)(2,1)S(1)}, bf16[512,256]{0,1:T(8,128)(2,1)}, u32[]{:S(2)}) copy-start(bf16[512,256]{0,1:T(8,128)(2,1)} %copy.112) | copy-start | bytes 786436
  219.1 18.4 %copy-start.2 = (bf16[1,128,1024]{2,1,0:T(8,128)(2,1)S(1)}, bf16[1,128,1024]{2,1,0:T(8,128)(2,1)}, u32[]{:S(2)}) copy-start(bf16[1,128,1024]{2,1,0:T(8,128)(2,1)} %param.11) | copy-start | bytes 786436
  219.1 20.1 %copy-start.8 = (f32[1024]{0:T(1024)S(1)}, f32[1024]{0:T(1024)}, u32[]{:S(2)}) copy-start(f32[1024]{0:T(1024)} %param.19) | copy-start | bytes 12292
  254.1 135.6 %all-to-all-start = ((bf16[32,40,1024]{2,1,0:T(8,128)(2,1)}), bf16[32,40,1024]{2,1,0:T(8,128)(2,1)S(1)}, u32[]{:S(2)}, u32[]{:S(2)}) async-start(bf16[32,40,1024]{2,1,0:T(8,128)(2,1)} %bitcast.31), calls=%async_computation | async-start | bytes 5242880 | tf_op jit(solution)/shard_map/all_to_all | solution.py:162
  266.9 62.5 %all-gather.13.cloned.1.call-start = ((), (), s32[]{:S(2)}) async-start(), calls=%async_computation.5 | async-start | bytes 2228224 | tf_op jit(solution)/shard_map/all_gather | solution.py:169
  267.5 128.3 %all-gather.15.cloned.1.call-start = ((), (), s32[]{:S(2)}) async-start(), calls=%async_computation.6 | async-start | bytes 1114112 | tf_op jit(solution)/shard_map/all_gather | solution.py:177
  437.4 6.9 %copy-start.9 = (f32[1,128,8]{1,2,0:T(8,128)S(1)}, f32[1,128,8]{1,2,0:T(8,128)}, u32[]{:S(2)}) copy-start(f32[1,128,8]{1,2,0:T(8,128)} %param.15) | copy-start | bytes 12292
  437.4 129.7 %all-to-all-start.1 = ((bf16[32,2,20480]{2,1,0:T(2,128)(2,1)}), bf16[32,2,20480]{2,1,0:T(2,128)(2,1)S(1)}, u32[]{:S(2)}, u32[]{:S(2)}) async-start(bf16[32,2,20480]{2,1,0:T(2,128)(2,1)} %reshape.386), calls=%async_computation.1 | async-start | bytes 5242880 | tf_op jit(solution)/shard_map/all_to_all | solution.py:180
Sparse Core Ops, SparseCore 0:
  43.2 58.0 all-gather.6
  105.4 73.6 all-gather.8
  182.1 55.3 all-gather.10
  270.4 58.9 all-gather.12
  332.3 57.4 all-gather.14
where the time goes:
time: 594 us; the launch traced here: 593 us
  waiting for transfers between devices  317 us (53%)
  blocking collectives  96.7 us (16%)
  local copies, waits for them, and re-layouts  74.3 us (13%)
  other arithmetic  38.8 us (7%)
  matrix products  32.4 us (5%)
  starting transfers between devices  19.9 us (3%)
  between operations  14.2 us (2%)
    all_to_all x1, waiting for transfers between devices, local(): lax.all_to_all(expert_result, 'tok', split_axis=1, concat_axis=0, tiled=T...  123 us
    all_gather x1, waiting for transfers between devices, local(): lax.all_gather(expert_gate_up, 'grp', axis=1, tiled=True)  61.4 us
    all_to_all x1, waiting for transfers between devices, local(): lax.all_to_all(outgoing.reshape(EXPERTS, CAP, model_width), 'tok', split_...  60.2 us
    all_gather x1, waiting for transfers between devices, local(): lax.all_gather(columns, 'grp', axis=0, tiled=True)  55.2 us
    all_gather x1, blocking collectives, local(): columns = lax.all_gather(w_qkv, 'tok', axis=1, tiled=True)  35 us
    all_gather x1, blocking collectives, local(): lax.all_gather(prefix_cache[0], 'tok', axis=0, tiled=True)  31 us
    all_gather x1, blocking collectives, local(): out_columns = lax.all_gather(w_out, 'tok', axis=1, tiled=True)  30.6 us
    convert_element_type x1, local copies, waits for them, and re-layouts, local(): expert_result = jnp.einsum('erf,efd->erd', sliced, lax.all_gather(expert_...  18.2 us
  transfers between devices with their start and end apart: 7, of which 5 were waited for; matrix products, arithmetic and copies ran while one was open for 10% of the time, Pallas kernels for 0%

commit v1 on v0

--- a/solution.py
+++ b/solution.py
@@ -163,12 +163,37 @@
         outgoing.reshape(EXPERTS, CAP, model_width), "tok", split_axis=0, concat_axis=1, tiled=True
     )
     sliced = arrived
+    size, here, span = (lax.axis_size("grp"), lax.axis_index("grp"), expert_gate_up.shape[1])
+    right = [(i, (i + 1) % size) for i in range(size)]
+    left = [(i, (i - 1) % size) for i in range(size)]
+    middle = size // 2
+    from_left = from_right = expert_gate_up
     hidden_pair = jnp.einsum(
         "erd,edf->erf",
-        sliced,
-        lax.all_gather(expert_gate_up, "grp", axis=1, tiled=True),
-        preferred_element_type=jnp.float32,
-    )
+        lax.dynamic_slice_in_dim(sliced, here * span, expert_gate_up.shape[1], axis=2),
+        expert_gate_up,
+        preferred_element_type=jnp.float32,
+    )
+    for step in range(1, middle + 1):
+        from_left = lax.ppermute(from_left, "grp", right)
+        if step < size - middle:
+            from_right = lax.ppermute(from_right, "grp", left)
+            hidden_pair = hidden_pair + jnp.einsum(
+                "erd,edf->erf",
+                lax.dynamic_slice_in_dim(
+                    sliced, (here + step) % size * span, from_right.shape[1], axis=2
+                ),
+                from_right,
+                preferred_element_type=jnp.float32,
+            )
+        hidden_pair = hidden_pair + jnp.einsum(
+            "erd,edf->erf",
+            lax.dynamic_slice_in_dim(
+                sliced, (here - step) % size * span, from_left.shape[1], axis=2
+            ),
+            from_left,
+            preferred_element_type=jnp.float32,
+        )
     activated = (jax.nn.silu(hidden_pair[..., :FF]) * hidden_pair[..., FF:]).astype(jnp.bfloat16)
     sliced = activated
     expert_result = jnp.einsum(

time: 594 us -> 669 us (1.13)
  matrix products: 32.4 us -> 106 us
  waiting for transfers between devices: 317 us -> 244 us
  starting transfers between devices: 19.9 us -> 83.4 us
    dot_general x1 -> x16, matrix products: 6.17 us -> 80.3 us  [the longest x8 51.8 us: local(): jnp.einsum('erd,edf->erf', lax.dynamic_slice_in_dim(sliced, (here - step)...]
    ppermute x0 -> x15, starting transfers between devices: none -> 66.3 us  [the longest x7 49.8 us: local(): from_right = lax.ppermute(from_right, 'grp', left)]
    all_gather x1 -> x0, waiting for transfers between devices: 61.4 us -> none  [local(): lax.all_gather(expert_gate_up, 'grp', axis=1, tiled=True)]
    all_to_all x1, waiting for transfers between devices: 60.2 us -> 48.4 us  [local(): lax.all_to_all(outgoing.reshape(EXPERTS, CAP, model_width), 'tok', split_...]
    ppermute x0 -> x15, waiting for transfers between devices: none -> 7.44 us  [the longest x8 7.43 us: local(): from_left = lax.ppermute(from_left, 'grp', right)]
    unnamed x26 -> x56, local copies, waits for them, and re-layouts: 17.1 us -> 16.3 us
  transfers between devices with their start and end apart: 7 -> 21, of which waited for: 5 -> 11; matrix products, arithmetic and copies ran while one was open for 10% -> 21% of each run, Pallas kernels for 0% -> 0%
where the time goes in v1:
time: 669 us; the launch traced here: 664 us
  waiting for transfers between devices  244 us (36%)
  matrix products  106 us (16%)
  blocking collectives  96.6 us (14%)
  starting transfers between devices  83.4 us (12%)
  local copies, waits for them, and re-layouts  80.5 us (12%)
  other arithmetic  38.6 us (6%)
  between operations  15 us (2%)
    all_to_all x1, waiting for transfers between devices, local(): lax.all_to_all(expert_result, 'tok', split_axis=1, concat_axis=0, tiled=T...  122 us
    all_gather x1, waiting for transfers between devices, local(): lax.all_gather(columns, 'grp', axis=0, tiled=True)  55.2 us
    dot_general x8, matrix products, local(): jnp.einsum('erd,edf->erf', lax.dynamic_slice_in_dim(sliced, (here - step)...  51.8 us
    ppermute x7, starting transfers between devices, local(): from_right = lax.ppermute(from_right, 'grp', left)  49.8 us
    all_to_all x1, waiting for transfers between devices, local(): lax.all_to_all(outgoing.reshape(EXPERTS, CAP, model_width), 'tok', split_...  48.4 us
    all_gather x1, blocking collectives, local(): columns = lax.all_gather(w_qkv, 'tok', axis=1, tiled=True)  35 us
    all_gather x1, blocking collectives, local(): lax.all_gather(prefix_cache[0], 'tok', axis=0, tiled=True)  31 us
    all_gather x1, blocking collectives, local(): out_columns = lax.all_gather(w_out, 'tok', axis=1, tiled=True)  30.6 us
  transfers between devices with their start and end apart: 21, of which 11 were waited for; matrix products, arithmetic and copies ran while one was open for 21% of the time, Pallas kernels for 0%

profile of v1, /device:TPU:32, one launch (start us, length us, event | category | flops | bytes accessed | tf_op | source)
XLA Modules:
  0.0 663.7 jit_solution(2571721629034677518)
XLA Ops:
  7.2 35.0 %all_gather.21 = bf16[64,1024]{0,1:T(8,128)(2,1)S(1)} all-gather(bf16[64,32]{0,1:T(8,128)(2,1)} %param.17), channel_id=1, replica_groups=mesh['grp'=16,'tok'=32] {'tok'}, dimensions={1}, use_global_device_ids=true | all-gather | bytes 135168 | tf_op jit(solution)/shard_map/all_gather | solution.py:101
  46.1 55.2 %all-gather.6.cloned.1.call-done = bf16[1024,1024]{1,0:T(8,128)(2,1)} async-done(((bf16[64,1024]{1,0:T(8,128)(2,1)}), bf16[1024,1024]{1,0:T(8,128)(2,1)}) %all-gather.6.cloned.1.call-update) | async-done | bytes 2097168 | tf_op jit(solution)/shard_map/all_gather | solution.py:105
  104.7 30.6 %all_gather.25 = bf16[32,1024]{0,1:T(8,128)(2,1)S(1)} all-gather(bf16[32,32]{0,1:T(8,128)(2,1)S(1)} %copy.120), channel_id=1, replica_groups=mesh['grp'=16,'tok'=32] {'tok'}, dimensions={1}, use_global_device_ids=true | all-gather | bytes 67584 | tf_op jit(solution)/shard_map/all_gather | solution.py:140
  140.8 5.4 broadcast_in_dim.42
  146.2 31.0 %all-gather = bf16[1,512,512]{2,1,0:T(8,128)(2,1)S(1)} all-gather(bf16[1,16,512]{2,1,0:T(8,128)(2,1)S(1)} %copy-done.20), channel_id=2, replica_groups=mesh['grp'=16,'tok'=32] {'tok'}, dimensions={1}, use_global_device_ids=true | all-gather | bytes 540672 | tf_op jit(solution)/shard_map/all_gather | solution.py:129
  177.6 9.0 %reduce-window.11 = s32[32,8,128]{2,1,0:T(8,128)S(1)} reduce-window(s32[32,8,128]{2,1,0:T(8,128)S(1)} %fusion.99, s32[]{:T(128)} %constant.147.clone.1), window={size=1x1x128 pad=0_0x0_0x127_0}, to_apply=%region_9.10 | reduce-window | flops 4161536 | bytes 262148 | tf_op jit(solution)/shard_map/reduce-window.1
  190.4 4.5 fusion.123
  194.8 4.1 copy.115
  199.0 4.1 copy.117
  203.1 4.7 fusion
  207.8 4.4 fusion.1
  214.7 8.6 %fusion.3 = f32[4,256,64]{1,2,0:T(8,128)S(1)} fusion(bf16[4,4096,64]{1,2,0:T(8,128)(2,1)} %bitcast.213, f32[4,256,4096]{2,1,0:T(8,128)} %copy-done, f32[4,256]{1,0:T(4,128)S(1)} %get-tuple-element.15, pred[256,4096]{1,0:T(8,128)(4,1)S(1)} %broadcast_in_dim.42), kind=kOutput, calls=%fused_computation.8 | convolution fusion | flops 553648128 | bytes 20189184 | tf_op jit(solution)/shard_map/kqn,knd->kqd/dot_general | solution.py:70
  225.9 10.4 %all-gather.10.cloned.1.call-done = bf16[512,1024]{1,0:T(8,128)(2,1)} async-done(((bf16[32,1024]{1,0:T(8,128)(2,1)}), bf16[512,1024]{1,0:T(8,128)(2,1)}) %all-gather.10.cloned.1.call-update) | async-done | bytes 1048592 | tf_op jit(solution)/shard_map/all_gather | solution.py:144
  238.1 15.0 %scatter_custom_fusion = bf16[1280,1024]{1,0:T(8,128)(2,1)} fusion(s32[1024]{0:T(1024)S(1)} %bitcast.226, bf16[128,1024]{1,0:T(8,128)(2,1)S(1)} %multiply_convert_fusion, s32[1024]{0:T(1024)S(1)} %broadcast_clamp_fusion.1, bf16[]{:T(256)} %constant.153.clone.1), kind=kCustom, calls=%fused_computation.18 | custom fusion | bytes 2621442 | tf_op jit(solution)/shard_map/scatter | solution.py:160
  253.1 12.9 %all-to-all-start = ((bf16[32,40,1024]{2,1,0:T(8,128)(2,1)}), bf16[32,40,1024]{2,1,0:T(8,128)(2,1)S(1)}, u32[]{:S(2)}, u32[]{:S(2)}) async-start(bf16[32,40,1024]{2,1,0:T(8,128)(2,1)} %bitcast.210), calls=%async_computation | async-start | bytes 5242880 | tf_op jit(solution)/shard_map/all_to_all | solution.py:162
  269.1 6.2 collective-permute-start
  278.8 7.2 %collective-permute-start.2 = (bf16[1,64,1024]{2,1,0:T(8,128)(2,1)S(1)}, bf16[1,64,1024]{2,1,0:T(8,128)(2,1)S(1)}, u32[]{:S(2)}, u32[]{:S(2)}) collective-permute-start(bf16[1,64,1024]{2,1,0:T(8,128)(2,1)S(1)} %collective-permute-done), channel_id=1, source_target_pairs={{0,480},{32,0},{64,32},{96,64},{128,96},{160,128},{192,160},{224,1... | collective-permute-start | bytes 393224 | tf_op jit(solution)/shard_map/ppermute | solution.py:180
  289.0 7.2 %collective-permute-start.4 = (bf16[1,64,1024]{2,1,0:T(8,128)(2,1)S(1)}, bf16[1,64,1024]{2,1,0:T(8,128)(2,1)S(1)}, u32[]{:S(2)}, u32[]{:S(2)}) collective-permute-start(bf16[1,64,1024]{2,1,0:T(8,128)(2,1)S(1)} %collective-permute-done.2), channel_id=1, source_target_pairs={{0,480},{32,0},{64,32},{96,64},{128,96},{160,128},{192,160},{224,1... | collective-permute-start | bytes 393224 | tf_op jit(solution)/shard_map/ppermute | solution.py:180
  299.2 7.2 %collective-permute-start.6 = (bf16[1,64,1024]{2,1,0:T(8,128)(2,1)S(1)}, bf16[1,64,1024]{2,1,0:T(8,128)(2,1)S(1)}, u32[]{:S(2)}, u32[]{:S(2)}) collective-permute-start(bf16[1,64,1024]{2,1,0:T(8,128)(2,1)S(1)} %collective-permute-done.4), channel_id=1, source_target_pairs={{0,480},{32,0},{64,32},{96,64},{128,96},{160,128},{192,160},{224,1... | collective-permute-start | bytes 393224 | tf_op jit(solution)/shard_map/ppermute | solution.py:180
  309.4 7.2 %collective-permute-start.8 = (bf16[1,64,1024]{2,1,0:T(8,128)(2,1)S(1)}, bf16[1,64,1024]{2,1,0:T(8,128)(2,1)}, u32[]{:S(2)}, u32[]{:S(2)}) collective-permute-start(bf16[1,64,1024]{2,1,0:T(8,128)(2,1)S(1)} %collective-permute-done.6), channel_id=1, source_target_pairs={{0,480},{32,0},{64,32},{96,64},{128,96},{160,128},{192,160},{224,1... | collective-permute-start | bytes 393224 | tf_op jit(solution)/shard_map/ppermute | solution.py:180
  319.6 7.4 %collective-permute-start.10 = (bf16[1,64,1024]{2,1,0:T(8,128)(2,1)}, bf16[1,64,1024]{2,1,0:T(8,128)(2,1)}, u32[]{:S(2)}, u32[]{:S(2)}) collective-permute-start(bf16[1,64,1024]{2,1,0:T(8,128)(2,1)} %collective-permute-done.8), channel_id=1, source_target_pairs={{0,480},{32,0},{64,32},{96,64},{128,96},{160,128},{192,160},{224,1... | collective-permute-start | bytes 393224 | tf_op jit(solution)/shard_map/ppermute | solution.py:180
  330.1 7.3 %collective-permute-start.12 = (bf16[1,64,1024]{2,1,0:T(8,128)(2,1)}, bf16[1,64,1024]{2,1,0:T(8,128)(2,1)}, u32[]{:S(2)}, u32[]{:S(2)}) collective-permute-start(bf16[1,64,1024]{2,1,0:T(8,128)(2,1)} %collective-permute-done.10), channel_id=1, source_target_pairs={{0,480},{32,0},{64,32},{96,64},{128,96},{160,128},{192,160},{224,1... | collective-permute-start | bytes 393224 | tf_op jit(solution)/shard_map/ppermute | solution.py:180
  340.5 48.4 %all-to-all-done = bf16[32,40,1024]{2,1,0:T(8,128)(2,1)S(1)} async-done(((bf16[32,40,1024]{2,1,0:T(8,128)(2,1)}), bf16[32,40,1024]{2,1,0:T(8,128)(2,1)S(1)}, u32[]{:S(2)}, u32[]{:S(2)}) %all-to-all-start) | async-done | bytes 2621472 | tf_op jit(solution)/shard_map/all_to_all | solution.py:162
  396.2 4.2 fusion.35
  403.5 4.1 fusion.39
  441.6 27.6 %add_bitcast_fusion = f32[1,1280,1024]{2,1,0:T(8,128)} fusion(f32[1280,1024]{1,0:T(8,128)} %fusion.29, f32[1280,1024]{1,0:T(8,128)} %fusion.31, f32[1280,1024]{1,0:T(8,128)} %fusion.33, f32[1280,1024]{1,0:T(8,128)} %fusion.35, f32[1280,1024]{1,0:T(8,128)} %fusion.37, f32[1280,1024]{1,0:T(8,128)} %fusion.39, f32[1280,1024]{1,0:T(8,128)} %fusion.41, ...), kind=kOutput, calls=%fused_computation.10 | convolution fusion | flops 187432960 | bytes 84344832 | tf_op jit(solution)/shard_map/erd,edf->erf/dot_general | solution.py:189
  469.2 4.4 fusion.7
  473.6 18.2 %copy.137 = bf16[1,1280,1024]{2,0,1:T(2,128)(2,1)} copy(bf16[1,1280,1024]{2,1,0:T(8,128)(2,1)S(1)} %fusion.7) | data formatting | bytes 5242880 | tf_op jit(solution)/shard_map/convert_element_type | solution.py:204
  492.3 15.6 %reduce = bf16[1280,1024]{1,0:T(8,128)(2,1)S(1)} reduce(bf16[1280,1,1024]{2,1,0:T(2,128)(2,1)} %bitcast.207, bf16[]{:T(256)} %broadcast.312), dimensions={1}, to_apply=%bitcast.189.reduce_sub_computation | reduce | bytes 5242882
  515.0 122.2 %all-to-all-done.1 = bf16[32,2,20480]{2,1,0:T(2,128)(2,1)S(1)} async-done(((bf16[32,2,20480]{2,1,0:T(2,128)(2,1)}), bf16[32,2,20480]{2,1,0:T(2,128)(2,1)S(1)}, u32[]{:S(2)}, u32[]{:S(2)}) %all-to-all-start.1) | async-done | bytes 2621472 | tf_op jit(solution)/shard_map/all_to_all | solution.py:205
  637.2 7.2 %reshape.536 = bf16[1280,1,1024]{2,1,0:T(2,128)(2,1)} reshape(bf16[32,2,20480]{2,1,0:T(2,128)(2,1)S(1)} %all-to-all-done.1) | data formatting | bytes 5242880
  647.9 5.4 gather_fusion
  (165 shorter events, 106.5 us)
Async XLA Ops:
  7.2 94.1 %all-gather.6.cloned.1.call-start = ((), (), s32[]{:S(2)}) async-start(), calls=%async_computation.2 | async-start | bytes 2228224 | tf_op jit(solution)/shard_map/all_gather | solution.py:105
  42.3 62.3 %copy-start.22 = (bf16[32,32]{1,0:T(8,128)(2,1)S(1)}, bf16[32,32]{1,0:T(8,128)(2,1)}, u32[]{:S(2)}) copy-start(bf16[32,32]{1,0:T(8,128)(2,1)} %param.18) | copy-start | bytes 6148
  43.1 147.3 %all-gather.8.cloned.1.call-start = ((), (), s32[]{:S(2)}) async-start(), calls=%async_computation.3 | async-start | bytes 4325376 | tf_op jit(solution)/shard_map/all_gather | solution.py:131
  46.0 90.1 %copy-start.21 = (s32[1,128,8]{1,2,0:T(8,128)S(1)}, s32[1,128,8]{1,2,0:T(8,128)}, u32[]{:S(2)}) copy-start(s32[1,128,8]{1,2,0:T(8,128)} %param.14) | copy-start | bytes 12292
  104.5 131.8 %all-gather.10.cloned.1.call-start = ((), (), s32[]{:S(2)}) async-start(), calls=%async_computation.4 | async-start | bytes 1114112 | tf_op jit(solution)/shard_map/all_gather | solution.py:144
  137.0 9.2 %copy-start.20 = (bf16[1,16,512]{2,1,0:T(8,128)(2,1)S(1)}, bf16[1,16,512]{2,1,0:T(8,128)(2,1)}, u32[]{:S(2)}) copy-start(bf16[1,16,512]{2,1,0:T(8,128)(2,1)} %param.13) | copy-start | bytes 49156
  207.8 6.3 copy-start
  223.3 13.0 %copy-start.2 = (bf16[1,128,1024]{2,1,0:T(8,128)(2,1)S(1)}, bf16[1,128,1024]{2,1,0:T(8,128)(2,1)}, u32[]{:S(2)}) copy-start(bf16[1,128,1024]{2,1,0:T(8,128)(2,1)} %param.11) | copy-start | bytes 786436
  223.3 14.7 %copy-start.23 = (f32[1024]{0:T(1024)S(1)}, f32[1024]{0:T(1024)}, u32[]{:S(2)}) copy-start(f32[1024]{0:T(1024)} %param.19) | copy-start | bytes 12292
  253.1 13.0 %copy-start.3 = (bf16[1,64,1024]{2,1,0:T(8,128)(2,1)S(1)}, bf16[1,64,1024]{2,1,0:T(8,128)(2,1)}, u32[]{:S(2)}) copy-start(bf16[1,64,1024]{2,1,0:T(8,128)(2,1)} %param.20) | copy-start | bytes 393220
  253.1 135.7 %all-to-all-start = ((bf16[32,40,1024]{2,1,0:T(8,128)(2,1)}), bf16[32,40,1024]{2,1,0:T(8,128)(2,1)S(1)}, u32[]{:S(2)}, u32[]{:S(2)}) async-start(bf16[32,40,1024]{2,1,0:T(8,128)(2,1)} %bitcast.210), calls=%async_computation | async-start | bytes 5242880 | tf_op jit(solution)/shard_map/all_to_all | solution.py:162
  266.1 203.1 %all-gather.12.cloned.1.call-start = ((), (), s32[]{:S(2)}) async-start(), calls=%async_computation.5 | async-start | bytes 1114112 | tf_op jit(solution)/shard_map/all_gather | solution.py:202
  266.1 10.8 %collective-permute-start.1 = (bf16[1,64,1024]{2,1,0:T(8,128)(2,1)S(1)}, bf16[1,64,1024]{2,1,0:T(8,128)(2,1)S(1)}, u32[]{:S(2)}, u32[]{:S(2)}) collective-permute-start(bf16[1,64,1024]{2,1,0:T(8,128)(2,1)S(1)} %copy-done.3), channel_id=1, source_target_pairs={{0,32},{32,64},{64,96},{96,128},{128,160},{160,192},{192,224},{224... | collective-permute-start | bytes 393224 | tf_op jit(solution)/shard_map/ppermute | solution.py:178
  269.1 9.7 %collective-permute-start = (bf16[1,64,1024]{2,1,0:T(8,128)(2,1)S(1)}, bf16[1,64,1024]{2,1,0:T(8,128)(2,1)S(1)}, u32[]{:S(2)}, u32[]{:S(2)}) collective-permute-start(bf16[1,64,1024]{2,1,0:T(8,128)(2,1)S(1)} %copy-done.3), channel_id=1, source_target_pairs={{0,480},{32,0},{64,32},{96,64},{128,96},{160,128},{192,160},{224,1... | collective-permute-start | bytes 393224 | tf_op jit(solution)/shard_map/ppermute | solution.py:180
  276.9 10.2 %collective-permute-start.3 = (bf16[1,64,1024]{2,1,0:T(8,128)(2,1)S(1)}, bf16[1,64,1024]{2,1,0:T(8,128)(2,1)S(1)}, u32[]{:S(2)}, u32[]{:S(2)}) collective-permute-start(bf16[1,64,1024]{2,1,0:T(8,128)(2,1)S(1)} %collective-permute-done.1), channel_id=1, source_target_pairs={{0,32},{32,64},{64,96},{96,128},{128,160},{160,192},{192,224},{224... | collective-permute-start | bytes 393224 | tf_op jit(solution)/shard_map/ppermute | solution.py:178
  278.8 58.6 %copy-start.4 = (bf16[1,64,1024]{2,1,0:T(8,128)(2,1)}, bf16[1,64,1024]{2,1,0:T(8,128)(2,1)S(1)}, u32[]{:S(2)}) copy-start(bf16[1,64,1024]{2,1,0:T(8,128)(2,1)S(1)} %collective-permute-done) | copy-start | bytes 393220
  278.8 10.2 %collective-permute-start.2 = (bf16[1,64,1024]{2,1,0:T(8,128)(2,1)S(1)}, bf16[1,64,1024]{2,1,0:T(8,128)(2,1)S(1)}, u32[]{:S(2)}, u32[]{:S(2)}) collective-permute-start(bf16[1,64,1024]{2,1,0:T(8,128)(2,1)S(1)} %collective-permute-done), channel_id=1, source_target_pairs={{0,480},{32,0},{64,32},{96,64},{128,96},{160,128},{192,160},{224,1... | collective-permute-start | bytes 393224 | tf_op jit(solution)/shard_map/ppermute | solution.py:180
  287.1 10.2 %collective-permute-start.5 = (bf16[1,64,1024]{2,1,0:T(8,128)(2,1)S(1)}, bf16[1,64,1024]{2,1,0:T(8,128)(2,1)S(1)}, u32[]{:S(2)}, u32[]{:S(2)}) collective-permute-start(bf16[1,64,1024]{2,1,0:T(8,128)(2,1)S(1)} %collective-permute-done.3), channel_id=1, source_target_pairs={{0,32},{32,64},{64,96},{96,128},{128,160},{160,192},{192,224},{224... | collective-permute-start | bytes 393224 | tf_op jit(solution)/shard_map/ppermute | solution.py:178
  289.0 8.2 %copy-start.8 = (bf16[1,64,1024]{2,1,0:T(8,128)(2,1)}, bf16[1,64,1024]{2,1,0:T(8,128)(2,1)S(1)}, u32[]{:S(2)}) copy-start(bf16[1,64,1024]{2,1,0:T(8,128)(2,1)S(1)} %collective-permute-done.2) | copy-start | bytes 393220
  289.0 10.1 %collective-permute-start.4 = (bf16[1,64,1024]{2,1,0:T(8,128)(2,1)S(1)}, bf16[1,64,1024]{2,1,0:T(8,128)(2,1)S(1)}, u32[]{:S(2)}, u32[]{:S(2)}) collective-permute-start(bf16[1,64,1024]{2,1,0:T(8,128)(2,1)S(1)} %collective-permute-done.2), channel_id=1, source_target_pairs={{0,480},{32,0},{64,32},{96,64},{128,96},{160,128},{192,160},{224,1... | collective-permute-start | bytes 393224 | tf_op jit(solution)/shard_map/ppermute | solution.py:180
  297.3 10.2 %collective-permute-start.7 = (bf16[1,64,1024]{2,1,0:T(8,128)(2,1)S(1)}, bf16[1,64,1024]{2,1,0:T(8,128)(2,1)S(1)}, u32[]{:S(2)}, u32[]{:S(2)}) collective-permute-start(bf16[1,64,1024]{2,1,0:T(8,128)(2,1)S(1)} %collective-permute-done.5), channel_id=1, source_target_pairs={{0,32},{32,64},{64,96},{96,128},{128,160},{160,192},{192,224},{224... | collective-permute-start | bytes 393224 | tf_op jit(solution)/shard_map/ppermute | solution.py:178
  299.2 8.2 %copy-start.12 = (bf16[1,64,1024]{2,1,0:T(8,128)(2,1)}, bf16[1,64,1024]{2,1,0:T(8,128)(2,1)S(1)}, u32[]{:S(2)}) copy-start(bf16[1,64,1024]{2,1,0:T(8,128)(2,1)S(1)} %collective-permute-done.4) | copy-start | bytes 393220
  299.2 10.1 %collective-permute-start.6 = (bf16[1,64,1024]{2,1,0:T(8,128)(2,1)S(1)}, bf16[1,64,1024]{2,1,0:T(8,128)(2,1)S(1)}, u32[]{:S(2)}, u32[]{:S(2)}) collective-permute-start(bf16[1,64,1024]{2,1,0:T(8,128)(2,1)S(1)} %collective-permute-done.4), channel_id=1, source_target_pairs={{0,480},{32,0},{64,32},{96,64},{128,96},{160,128},{192,160},{224,1... | collective-permute-start | bytes 393224 | tf_op jit(solution)/shard_map/ppermute | solution.py:180
  307.4 10.2 %collective-permute-start.9 = (bf16[1,64,1024]{2,1,0:T(8,128)(2,1)S(1)}, bf16[1,64,1024]{2,1,0:T(8,128)(2,1)S(1)}, u32[]{:S(2)}, u32[]{:S(2)}) collective-permute-start(bf16[1,64,1024]{2,1,0:T(8,128)(2,1)S(1)} %collective-permute-done.7), channel_id=1, source_target_pairs={{0,32},{32,64},{64,96},{96,128},{128,160},{160,192},{192,224},{224... | collective-permute-start | bytes 393224 | tf_op jit(solution)/shard_map/ppermute | solution.py:178
  309.4 8.2 %copy-start.16 = (bf16[1,64,1024]{2,1,0:T(8,128)(2,1)}, bf16[1,64,1024]{2,1,0:T(8,128)(2,1)S(1)}, u32[]{:S(2)}) copy-start(bf16[1,64,1024]{2,1,0:T(8,128)(2,1)S(1)} %collective-permute-done.6) | copy-start | bytes 393220
  309.4 10.1 %collective-permute-start.8 = (bf16[1,64,1024]{2,1,0:T(8,128)(2,1)S(1)}, bf16[1,64,1024]{2,1,0:T(8,128)(2,1)}, u32[]{:S(2)}, u32[]{:S(2)}) collective-permute-start(bf16[1,64,1024]{2,1,0:T(8,128)(2,1)S(1)} %collective-permute-done.6), channel_id=1, source_target_pairs={{0,480},{32,0},{64,32},{96,64},{128,96},{160,128},{192,160},{224,1... | collective-permute-start | bytes 393224 | tf_op jit(solution)/shard_map/ppermute | solution.py:180
  317.6 10.3 %collective-permute-start.11 = (bf16[1,64,1024]{2,1,0:T(8,128)(2,1)S(1)}, bf16[1,64,1024]{2,1,0:T(8,128)(2,1)}, u32[]{:S(2)}, u32[]{:S(2)}) collective-permute-start(bf16[1,64,1024]{2,1,0:T(8,128)(2,1)S(1)} %collective-permute-done.9), channel_id=1, source_target_pairs={{0,32},{32,64},{64,96},{96,128},{128,160},{160,192},{192,224},{224... | collective-permute-start | bytes 393224 | tf_op jit(solution)/shard_map/ppermute | solution.py:178
  319.6 10.6 %collective-permute-start.10 = (bf16[1,64,1024]{2,1,0:T(8,128)(2,1)}, bf16[1,64,1024]{2,1,0:T(8,128)(2,1)}, u32[]{:S(2)}, u32[]{:S(2)}) collective-permute-start(bf16[1,64,1024]{2,1,0:T(8,128)(2,1)} %collective-permute-done.8), channel_id=1, source_target_pairs={{0,480},{32,0},{64,32},{96,64},{128,96},{160,128},{192,160},{224,1... | collective-permute-start | bytes 393224 | tf_op jit(solution)/shard_map/ppermute | solution.py:180
  327.9 10.5 %collective-permute-start.13 = (bf16[1,64,1024]{2,1,0:T(8,128)(2,1)}, bf16[1,64,1024]{2,1,0:T(8,128)(2,1)}, u32[]{:S(2)}, u32[]{:S(2)}) collective-permute-start(bf16[1,64,1024]{2,1,0:T(8,128)(2,1)} %collective-permute-done.11), channel_id=1, source_target_pairs={{0,32},{32,64},{64,96},{96,128},{128,160},{160,192},{192,224},{224... | collective-permute-start | bytes 393224 | tf_op jit(solution)/shard_map/ppermute | solution.py:178
  330.1 107.4 %collective-permute-start.12 = (bf16[1,64,1024]{2,1,0:T(8,128)(2,1)}, bf16[1,64,1024]{2,1,0:T(8,128)(2,1)}, u32[]{:S(2)}, u32[]{:S(2)}) collective-permute-start(bf16[1,64,1024]{2,1,0:T(8,128)(2,1)} %collective-permute-done.10), channel_id=1, source_target_pairs={{0,480},{32,0},{64,32},{96,64},{128,96},{160,128},{192,160},{224,1... | collective-permute-start | bytes 393224 | tf_op jit(solution)/shard_map/ppermute | solution.py:180
  338.4 103.2 %collective-permute-start.14 = (bf16[1,64,1024]{2,1,0:T(8,128)(2,1)}, bf16[1,64,1024]{2,1,0:T(8,128)(2,1)S(1)}, u32[]{:S(2)}, u32[]{:S(2)}) collective-permute-start(bf16[1,64,1024]{2,1,0:T(8,128)(2,1)} %collective-permute-done.13), channel_id=1, source_target_pairs={{0,32},{32,64},{64,96},{96,128},{128,160},{160,192},{192,224},{224... | collective-permute-start | bytes 393224 | tf_op jit(solution)/shard_map/ppermute | solution.py:178
  510.9 126.3 %all-to-all-start.1 = ((bf16[32,2,20480]{2,1,0:T(2,128)(2,1)}), bf16[32,2,20480]{2,1,0:T(2,128)(2,1)S(1)}, u32[]{:S(2)}, u32[]{:S(2)}) async-start(bf16[32,2,20480]{2,1,0:T(2,128)(2,1)} %reshape.535), calls=%async_computation.1 | async-start | bytes 5242880 | tf_op jit(solution)/shard_map/all_to_all | solution.py:205
  (14 other events, 45.6 us)
Sparse Core Ops, SparseCore 0:
  43.2 58.0 all-gather.5
  104.6 74.1 all-gather.7
  181.8 54.5 all-gather.9
  330.0 58.6 all-gather.11
